TPU v7x, 32 devices: a whole 2x2x4 slice. The times are simulated.
32 devices in a mesh: macro: 8 (over y, x, core), rve: 4 (over z).
Axes of the slice: x: 2, y: 2, z: 4, core: 2. Of those that a mesh axis runs over, the one named last changes fastest.
Arguments:
- deform: float32 [9, 512], P(None, 'macro'), may hold values from -6 to 6
- plastic: int32 [512], P('macro'), may hold values 0 or 1
- route: int32 [512], P('macro'), may hold values from 0 to 7, as said below
- stiff: float32 [8, 1536], P('macro', 'rve'), may hold values from 0.1 to 2
- cubic: float32 [8, 1536], P('macro', 'rve'), may hold values from 0.5 to 5
- coupling: float32 [8, 24, 2, 64, 64], P('macro', 'rve'), may hold values from -0.75 to 0.75
- conn: int32 [8, 24, 2], P('macro', 'rve'), may hold values from 0 to 5
- iface: float32 [8, 256, 64], P('macro', 'rve'), may hold values from -0.75 to 0.75
- load_map: float32 [8, 9, 1536], P('macro', None, 'rve'), may hold values from -2 to 2
- average_map: float32 [8, 9, 1536], P('macro', None, 'rve'), may hold values from -0.15625 to 0.15625
Outputs:
- stress: float32 [9, 512], P(None, 'macro')
- micro_field: float32 [8, 1536, 128], P('macro', 'rve')
Inputs may be any that keep to these rules, and one draw needn't show every extreme that they name: `route`: among the points of one macro section no group is named more than 16 times, and one group is named exactly 16 times by every section. `conn`: an index among the 6 blocks held with the same block row on one device.
All inputs are finite; a program needn't handle non-finite values. No bound on the sum of `plastic` on one device may be relied on, other than what follows from the above.
Results may differ from a plain program's by a relative error of at most 0.0003.
Values sent between devices are 32-bit elements; how exact they have to be, the bound alone decides.
A program may use at most 64 MiB of HBM per device.

v0:
```python
import jax
import jax.numpy as jnp
from jax import lax
from jax.sharding import PartitionSpec as P

ITERS = 2
NEWTON = 2
HIGHEST_PREC = lax.Precision.HIGHEST
EPSILON = 1e-06


def from_behind(block, axis, distance):
    devices = range(lax.axis_size(axis))
    route = [((i - distance) % len(devices), i) for i in devices]
    return lax.ppermute(block, axis, route)


def with_halo(block, sides, width):
    for axis, dim in sides:
        count = lax.axis_size(axis)
        forward = [(i, i + 1) for i in range(count - 1)]
        forward.append((count - 1, 0))
        backward = [(target, source) for source, target in forward]
        low = lax.ppermute(
            lax.slice_in_dim(block, block.shape[dim] - width, None, axis=dim), axis, forward
        )
        high = lax.ppermute(lax.slice_in_dim(block, 0, width, axis=dim), axis, backward)
        block = jnp.concatenate([low, block, high], axis=dim)
    return block


def slot_index(route_rows, capacity):
    point_count = route_rows.shape[0]
    position = jnp.arange(point_count, dtype=jnp.int32)
    same_group = route_rows[:, None] == route_rows[None, :]
    before = position[None, :] < position[:, None]
    rank_in = jnp.sum(
        jnp.where(jnp.logical_and(same_group, before), 1, 0).astype(jnp.int32), axis=1
    )
    return route_rows * capacity + rank_in


def local_matrix(coupling, conn, stiff):
    blocks, slot_count, block_size, _ = coupling.shape
    spring = jnp.einsum("bsxk,bsyk->bsxy", coupling, coupling, precision=HIGHEST_PREC)
    block_ids = jnp.arange(blocks, dtype=jnp.int32)
    own_mark = (block_ids[None, None, :] == block_ids[:, None, None]).astype(jnp.float32)
    far_mark = jnp.logical_and(
        block_ids[None, None, :] == conn[:, :, None], conn[:, :, None] != block_ids[:, None, None]
    ).astype(jnp.float32)
    weight = own_mark - far_mark
    pair_mark = jnp.einsum("bsk,bsl->bskl", weight, weight, precision=HIGHEST_PREC)
    assembled = jnp.einsum("bskl,bsxy->kxly", pair_mark, spring, precision=HIGHEST_PREC)
    assembled = assembled.reshape(blocks * block_size, blocks * block_size)
    return assembled + jnp.diag(stiff)


def norm_sum(values):
    return lax.psum(jnp.sum(values * values, axis=0), "rve")


def split_solve(strain, flag_cols, stiff, cubic, coupling, conn, iface, load_map):
    block_size = coupling.shape[3]
    local_part = local_matrix(coupling[0], conn[0], stiff[0])
    edge_block = iface[0]
    own_spring = jnp.einsum("xk,yk->xy", edge_block, edge_block, precision=HIGHEST_PREC)
    next_edge = from_behind(edge_block, "rve", -1)
    next_spring = jnp.einsum("xk,yk->xy", next_edge, next_edge, precision=HIGHEST_PREC)
    load_cols = jnp.einsum("ci,cp->ip", load_map[0], strain, precision=HIGHEST_PREC)
    hard = flag_cols * cubic[0][:, None]

    def operate(field):
        product = jnp.dot(
            local_part, field, precision=HIGHEST_PREC, preferred_element_type=jnp.float32
        )
        first_rows = field[:block_size]
        last_rows = field[-block_size:]
        end_rows = jnp.concatenate([first_rows, last_rows], axis=0)
        padded = with_halo(end_rows, (("rve", 0),), block_size)
        top_flux = jnp.dot(
            own_spring,
            first_rows - padded[:block_size],
            precision=HIGHEST_PREC,
            preferred_element_type=jnp.float32,
        )
        bottom = jnp.dot(
            next_spring,
            last_rows - padded[-block_size:],
            precision=HIGHEST_PREC,
            preferred_element_type=jnp.float32,
        )
        product = product.at[:block_size].add(top_flux)
        product = product.at[-block_size:].add(bottom)
        return product

    solution = jnp.zeros_like(load_cols)
    for newton_step in range(NEWTON):
        tangent_add = 3.0 * hard * solution * solution
        if newton_step == 0:
            right_side = load_cols
        else:
            right_side = load_cols - operate(solution) - hard * (solution * solution * solution)

        def sweep(turn_index, carried):
            iterate, residue, direct, norm_now = carried
            product = operate(direct) + tangent_add * direct
            curvature_col = lax.psum(jnp.sum(direct * product, axis=0), "rve")
            step_len = norm_now / (curvature_col + EPSILON)
            iterate = iterate + step_len * direct
            residue = residue - step_len * product
            norm_next = norm_sum(residue)
            direct = residue + norm_next / (norm_now + EPSILON) * direct
            return (iterate, residue, direct, norm_next)

        start = (jnp.zeros_like(right_side), right_side, right_side, norm_sum(right_side))
        iterate, residue, direct, norm_now = lax.fori_loop(0, ITERS, sweep, start)
        solution = solution + iterate
    return solution


def shards(deform, plastic, route, stiff, cubic, coupling, conn, iface, load_map, average_map):
    groups = lax.axis_size("macro")
    capacity = 2 * deform.shape[1] // groups
    columns = groups * capacity
    slot_ids = slot_index(route, capacity)
    places = jnp.arange(columns, dtype=jnp.int32)
    select = (slot_ids[:, None] == places[None, :]).astype(jnp.float32)
    outgoing = jnp.dot(
        deform, select, precision=HIGHEST_PREC, preferred_element_type=jnp.float32
    ).reshape(9, groups, capacity)
    flags_out = jnp.dot(
        plastic.astype(jnp.float32)[None, :],
        select,
        precision=HIGHEST_PREC,
        preferred_element_type=jnp.float32,
    ).reshape(1, groups, capacity)
    incoming, flags_in = (
        lax.all_to_all(outgoing, "macro", split_axis=1, concat_axis=1, tiled=True),
        lax.all_to_all(flags_out, "macro", split_axis=1, concat_axis=1, tiled=True),
    )
    strain = incoming.reshape(9, columns)
    flag_cols = flags_in.reshape(1, columns)
    solution = split_solve(strain, flag_cols, stiff, cubic, coupling, conn, iface, load_map)
    part_stress = jnp.einsum("ci,ip->cp", average_map[0], solution, precision=HIGHEST_PREC)
    group_stress = lax.psum(part_stress, "rve")
    returned_rows = lax.all_to_all(
        group_stress.reshape(9, groups, capacity), "macro", split_axis=1, concat_axis=1, tiled=True
    )
    stress = jnp.dot(
        returned_rows.reshape(9, columns),
        select.T,
        precision=HIGHEST_PREC,
        preferred_element_type=jnp.float32,
    )
    return (stress, solution[None])


def solution(mesh):
    return jax.shard_map(
        shards,
        mesh=mesh,
        in_specs=(
            P(None, "macro"),
            P("macro"),
            P("macro"),
            P("macro", "rve"),
            P("macro", "rve"),
            P("macro", "rve", None, None, None),
            P("macro", "rve", None),
            P("macro", "rve", None),
            P("macro", None, "rve"),
            P("macro", None, "rve"),
        ),
        out_specs=(P(None, "macro"), P("macro", "rve", None)),
        check_vma=False,
    )
```

profile of v0, /device:TPU:0, one launch (start us, length us, event | category | flops | bytes accessed | tf_op | source)
XLA Modules:
  0.0 195.9 jit_solution(6440798218701041127)
XLA Ops:
  2.2 1.7 fusion.23
  3.9 5.2 %all-to-all-start.1 = ((f32[1,8,16]{2,0,1:T(1,128)}), f32[1,8,16]{2,0,1:T(1,128)S(1)}, u32[]{:S(2)}, u32[]{:S(2)}) async-start(f32[1,8,16]{2,0,1:T(1,128)} %fusion.23), calls=%async_computation.1 | async-start | bytes 8192 | tf_op jit(solution)/shard_map/all_to_all | solution.py:139
  9.1 3.6 %collective-permute-start.4 = (f32[64,64]{1,0:T(8,128)}, f32[64,64]{1,0:T(8,128)S(1)}, u32[]{:S(2)}, u32[]{:S(2)}) collective-permute-start(f32[64,64]{1,0:T(8,128)} %bitcast.118), channel_id=1, source_target_pairs={{1,0},{2,1},{3,2},{0,3},{5,4},{6,5},{7,6},{4,7},{9,8},{10,9},{11,1... | collective-permute-start | bytes 49160 | tf_op jit(solution)/shard_map/ppermute | solution.py:15
  14.8 1.5 convolution_bitcast_fusion.4
  18.3 4.2 %all-to-all-start = ((f32[8,1,144]{2,1,0:T(1,128)}), f32[8,1,144]{2,1,0:T(1,128)S(1)}, u32[]{:S(2)}, u32[]{:S(2)}) async-start(f32[8,1,144]{2,1,0:T(1,128)} %reshape.256), calls=%async_computation | async-start | bytes 16384 | tf_op jit(solution)/shard_map/all_to_all | solution.py:138
  24.1 3.1 %all-to-all-done = f32[8,1,144]{2,1,0:T(1,128)S(1)} async-done(((f32[8,1,144]{2,1,0:T(1,128)}), f32[8,1,144]{2,1,0:T(1,128)S(1)}, u32[]{:S(2)}, u32[]{:S(2)}) %all-to-all-start) | async-done | bytes 4640 | tf_op jit(solution)/shard_map/all_to_all | solution.py:138
  29.3 8.8 %psum.65 = f32[128]{0:T(128)S(1)} all-reduce(f32[128]{0:T(128)S(1)} %get-tuple-element.577), channel_id=1, replica_groups=mesh['macro'=8,'rve'=4] {'rve'}, use_global_device_ids=true, to_apply=%region_2.3 | all-reduce | flops 128 | bytes 1024 | tf_op jit(solution)/shard_map/psum | solution.py:59
  38.3 54.1 %while.46 = (s32[]{:T(128)}, f32[384,128]{1,0:T(8,128)S(1)}, f32[384,128]{1,0:T(8,128)S(1)}, f32[384,128]{1,0:T(8,128)S(1)}, f32[128]{0:T(128)S(1)}, /*index=5*/...) while((s32[]{:T(128)}, f32[384,128]{1,0:T(8,128)S(1)}, ...), condition=%wide.region_8.9_spmd.clone, body=%wide.region_3.8_spmd.clone.sunk | while | flops 240042496 | bytes 3879119 | solution.py:116
  38.4 1.6 collective-permute-start
  40.0 2.3 %collective-permute-start.1 = (f32[64,128]{1,0:T(8,128)S(1)}, f32[64,128]{1,0:T(8,128)S(1)}, u32[]{:S(2)}, u32[]{:S(2)}) collective-permute-start(f32[64,128]{1,0:T(8,128)S(1)} %get-tuple-element.697), channel_id=1, source_target_pairs={{1,0},{2,1},{3,2},{0,3},{5,4},{6,5},{7,6},{4,7},{9,8},{10,9},{11,1... | collective-permute-start | bytes 98312 | tf_op jit(solution)/shard_map/while/body/eval_jaxpr/ppermute | solution.py:27
  42.9 1.3 collective-permute-done
  44.7 11.9 %psum.76 = f32[128]{0:T(128)S(1)} all-reduce(f32[128]{0:T(128)S(1)} %multiply_reduce_fusion.10), channel_id=1, replica_groups=mesh['macro'=8,'rve'=4] {'rve'}, use_global_device_ids=true, to_apply=%region_5.5 | all-reduce | flops 128 | bytes 1024 | tf_op jit(solution)/shard_map/while/body/eval_jaxpr/psum | solution.py:107
  56.9 8.4 %psum.77 = f32[128]{0:T(128)S(1)} all-reduce(f32[128]{0:T(128)S(1)} %get-tuple-element.700), channel_id=1, replica_groups=mesh['macro'=8,'rve'=4] {'rve'}, use_global_device_ids=true, to_apply=%region_7.7 | all-reduce | flops 128 | bytes 1024 | tf_op jit(solution)/shard_map/while/body/eval_jaxpr/psum | solution.py:59
  65.4 2.0 %collective-permute-start = (f32[64,128]{1,0:T(8,128)S(1)}, f32[64,128]{1,0:T(8,128)S(1)}, u32[]{:S(2)}, u32[]{:S(2)}) collective-permute-start(f32[64,128]{1,0:T(8,128)S(1)} %get-tuple-element.696), channel_id=1, source_target_pairs={{0,1},{1,2},{2,3},{3,0},{4,5},{5,6},{6,7},{7,4},{8,9},{9,10},{10,1... | collective-permute-start | bytes 98312 | tf_op jit(solution)/shard_map/while/body/eval_jaxpr/ppermute | solution.py:24
  67.4 1.9 collective-permute-start.1
  71.9 11.8 %psum.76 = f32[128]{0:T(128)S(1)} all-reduce(f32[128]{0:T(128)S(1)} %multiply_reduce_fusion.10), channel_id=1, replica_groups=mesh['macro'=8,'rve'=4] {'rve'}, use_global_device_ids=true, to_apply=%region_5.5 | all-reduce | flops 128 | bytes 1024 | tf_op jit(solution)/shard_map/while/body/eval_jaxpr/psum | solution.py:107
  84.0 8.4 %psum.77 = f32[128]{0:T(128)S(1)} all-reduce(f32[128]{0:T(128)S(1)} %get-tuple-element.700), channel_id=1, replica_groups=mesh['macro'=8,'rve'=4] {'rve'}, use_global_device_ids=true, to_apply=%region_7.7 | all-reduce | flops 128 | bytes 1024 | tf_op jit(solution)/shard_map/while/body/eval_jaxpr/psum | solution.py:59
  92.4 2.0 %collective-permute-start.5 = (f32[64,128]{1,0:T(8,128)S(1)}, f32[64,128]{1,0:T(8,128)S(1)}, u32[]{:S(2)}, u32[]{:S(2)}) collective-permute-start(f32[64,128]{1,0:T(8,128)S(1)} %get-tuple-element.576), channel_id=1, source_target_pairs={{0,1},{1,2},{2,3},{3,0},{4,5},{5,6},{6,7},{7,4},{8,9},{9,10},{10,1... | collective-permute-start | bytes 98312 | tf_op jit(solution)/shard_map/ppermute | solution.py:24
  95.3 1.9 collective-permute-start.6
  100.7 12.1 %psum.66 = f32[128]{0:T(128)S(1)} all-reduce(f32[128]{0:T(128)S(1)} %get-tuple-element.566), channel_id=1, replica_groups=mesh['macro'=8,'rve'=4] {'rve'}, use_global_device_ids=true, to_apply=%region_10.11 | all-reduce | flops 128 | bytes 1024 | tf_op jit(solution)/shard_map/psum | solution.py:59
  112.8 54.0 %while.47 = (s32[]{:T(128)}, f32[384,128]{1,0:T(8,128)S(1)}, f32[384,128]{1,0:T(8,128)S(1)}, f32[384,128]{1,0:T(8,128)S(1)}, f32[128]{0:T(128)S(1)}, /*index=5*/...) while((s32[]{:T(128)}, f32[384,128]{1,0:T(8,128)S(1)}, ...), condition=%wide.region_16.17_spmd.clone, body=%wide.region_11.16_spmd.clone.sunk | while | flops 239845888 | bytes 4268231 | solution.py:116
  112.9 3.8 %collective-permute-start.3 = (f32[64,128]{1,0:T(8,128)S(1)}, f32[64,128]{1,0:T(8,128)S(1)}, u32[]{:S(2)}, u32[]{:S(2)}) collective-permute-start(f32[64,128]{1,0:T(8,128)S(1)} %get-tuple-element.711), channel_id=1, source_target_pairs={{1,0},{2,1},{3,2},{0,3},{5,4},{6,5},{7,6},{4,7},{9,8},{10,9},{11,1... | collective-permute-start | bytes 98312 | tf_op jit(solution)/shard_map/while/body/eval_jaxpr/ppermute | solution.py:27
  119.0 12.0 %psum.78 = f32[128]{0:T(128)S(1)} all-reduce(f32[128]{0:T(128)S(1)} %multiply_reduce_fusion.12), channel_id=1, replica_groups=mesh['macro'=8,'rve'=4] {'rve'}, use_global_device_ids=true, to_apply=%region_13.13 | all-reduce | flops 128 | bytes 1024 | tf_op jit(solution)/shard_map/while/body/eval_jaxpr/psum | solution.py:107
  131.2 8.4 %psum.79 = f32[128]{0:T(128)S(1)} all-reduce(f32[128]{0:T(128)S(1)} %get-tuple-element.714), channel_id=1, replica_groups=mesh['macro'=8,'rve'=4] {'rve'}, use_global_device_ids=true, to_apply=%region_15.15 | all-reduce | flops 128 | bytes 1024 | tf_op jit(solution)/shard_map/while/body/eval_jaxpr/psum | solution.py:59
  139.7 2.0 %collective-permute-start.2 = (f32[64,128]{1,0:T(8,128)S(1)}, f32[64,128]{1,0:T(8,128)S(1)}, u32[]{:S(2)}, u32[]{:S(2)}) collective-permute-start(f32[64,128]{1,0:T(8,128)S(1)} %get-tuple-element.710), channel_id=1, source_target_pairs={{0,1},{1,2},{2,3},{3,0},{4,5},{5,6},{6,7},{7,4},{8,9},{9,10},{10,1... | collective-permute-start | bytes 98312 | tf_op jit(solution)/shard_map/while/body/eval_jaxpr/ppermute | solution.py:24
  141.7 1.9 collective-permute-start.3
  144.2 1.3 collective-permute-done.2
  146.3 11.9 %psum.78 = f32[128]{0:T(128)S(1)} all-reduce(f32[128]{0:T(128)S(1)} %multiply_reduce_fusion.12), channel_id=1, replica_groups=mesh['macro'=8,'rve'=4] {'rve'}, use_global_device_ids=true, to_apply=%region_13.13 | all-reduce | flops 128 | bytes 1024 | tf_op jit(solution)/shard_map/while/body/eval_jaxpr/psum | solution.py:107
  158.3 8.4 %psum.79 = f32[128]{0:T(128)S(1)} all-reduce(f32[128]{0:T(128)S(1)} %get-tuple-element.714), channel_id=1, replica_groups=mesh['macro'=8,'rve'=4] {'rve'}, use_global_device_ids=true, to_apply=%region_15.15 | all-reduce | flops 128 | bytes 1024 | tf_op jit(solution)/shard_map/while/body/eval_jaxpr/psum | solution.py:59
  167.2 18.3 %psum.67 = f32[9,8,16]{2,0,1:T(8,128)S(1)} all-reduce(f32[9,8,16]{2,0,1:T(8,128)S(1)} %copy.105), channel_id=1, replica_groups=mesh['macro'=8,'rve'=4] {'rve'}, use_global_device_ids=true, to_apply=%region_17.18 | all-reduce | flops 1152 | bytes 9216 | tf_op jit(solution)/shard_map/psum | solution.py:145
  186.2 3.3 %all-to-all-start.2 = ((f32[8,1,144]{2,1,0:T(1,128)}), f32[8,1,144]{2,1,0:T(1,128)S(1)}, u32[]{:S(2)}, u32[]{:S(2)}) async-start(f32[8,1,144]{2,1,0:T(1,128)} %reshape.258), calls=%async_computation.2 | async-start | bytes 16384 | tf_op jit(solution)/shard_map/all_to_all | solution.py:146
  190.2 3.9 %all-to-all-done.2 = f32[8,1,144]{2,1,0:T(1,128)S(1)} async-done(((f32[8,1,144]{2,1,0:T(1,128)}), f32[8,1,144]{2,1,0:T(1,128)S(1)}, u32[]{:S(2)}, u32[]{:S(2)}) %all-to-all-start.2) | async-done | bytes 4640 | tf_op jit(solution)/shard_map/all_to_all | solution.py:146
  (118 shorter events, 25.8 us)
Async XLA Ops:
  0.6 13.4 %copy-start = (f32[1,6,2,64,64]{4,3,2,1,0:T(8,128)S(1)}, f32[1,6,2,64,64]{4,3,2,1,0:T(8,128)}, u32[]{:S(2)}) copy-start(f32[1,6,2,64,64]{4,3,2,1,0:T(8,128)} %param.31) | copy-start | bytes 589828
  3.9 14.4 %all-to-all-start.1 = ((f32[1,8,16]{2,0,1:T(1,128)}), f32[1,8,16]{2,0,1:T(1,128)S(1)}, u32[]{:S(2)}, u32[]{:S(2)}) async-start(f32[1,8,16]{2,0,1:T(1,128)} %fusion.23), calls=%async_computation.1 | async-start | bytes 8192 | tf_op jit(solution)/shard_map/all_to_all | solution.py:139
  9.1 29.1 %collective-permute-start.4 = (f32[64,64]{1,0:T(8,128)}, f32[64,64]{1,0:T(8,128)S(1)}, u32[]{:S(2)}, u32[]{:S(2)}) collective-permute-start(f32[64,64]{1,0:T(8,128)} %bitcast.118), channel_id=1, source_target_pairs={{1,0},{2,1},{3,2},{0,3},{5,4},{6,5},{7,6},{4,7},{9,8},{10,9},{11,1... | collective-permute-start | bytes 49160 | tf_op jit(solution)/shard_map/ppermute | solution.py:15
  16.5 0.7 copy-start.4
  16.5 0.8 copy-start.6
  16.5 6.0 %copy-start.3 = (f32[1,64,64]{2,1,0:T(8,128)S(1)}, f32[1,64,64]{2,1,0:T(8,128)}, u32[]{:S(2)}) copy-start(f32[1,64,64]{2,1,0:T(8,128)} %param.33) | copy-start | bytes 49156
  16.5 6.2 %copy-start.5 = (f32[1,384]{1,0:T(1,128)S(1)}, f32[1,384]{1,0:T(1,128)}, u32[]{:S(2)}) copy-start(f32[1,384]{1,0:T(1,128)} %param.30) | copy-start | bytes 4612
  16.5 12.2 %copy-start.1 = (f32[1,9,384]{2,0,1:T(1,128)S(1)}, f32[1,9,384]{2,0,1:T(1,128)}, u32[]{:S(2)}) copy-start(f32[1,9,384]{2,0,1:T(1,128)} %param.34) | copy-start | bytes 41476
  18.3 8.9 %all-to-all-start = ((f32[8,1,144]{2,1,0:T(1,128)}), f32[8,1,144]{2,1,0:T(1,128)S(1)}, u32[]{:S(2)}, u32[]{:S(2)}) async-start(f32[8,1,144]{2,1,0:T(1,128)} %reshape.256), calls=%async_computation | async-start | bytes 16384 | tf_op jit(solution)/shard_map/all_to_all | solution.py:138
  38.4 5.8 %collective-permute-start = (f32[64,128]{1,0:T(8,128)S(1)}, f32[64,128]{1,0:T(8,128)S(1)}, u32[]{:S(2)}, u32[]{:S(2)}) collective-permute-start(f32[64,128]{1,0:T(8,128)S(1)} %get-tuple-element.696), channel_id=1, source_target_pairs={{0,1},{1,2},{2,3},{3,0},{4,5},{5,6},{6,7},{7,4},{8,9},{9,10},{10,1... | collective-permute-start | bytes 98312 | tf_op jit(solution)/shard_map/while/body/eval_jaxpr/ppermute | solution.py:24
  40.0 4.4 %collective-permute-start.1 = (f32[64,128]{1,0:T(8,128)S(1)}, f32[64,128]{1,0:T(8,128)S(1)}, u32[]{:S(2)}, u32[]{:S(2)}) collective-permute-start(f32[64,128]{1,0:T(8,128)S(1)} %get-tuple-element.697), channel_id=1, source_target_pairs={{1,0},{2,1},{3,2},{0,3},{5,4},{6,5},{7,6},{4,7},{9,8},{10,9},{11,1... | collective-permute-start | bytes 98312 | tf_op jit(solution)/shard_map/while/body/eval_jaxpr/ppermute | solution.py:27
  65.4 5.8 %collective-permute-start = (f32[64,128]{1,0:T(8,128)S(1)}, f32[64,128]{1,0:T(8,128)S(1)}, u32[]{:S(2)}, u32[]{:S(2)}) collective-permute-start(f32[64,128]{1,0:T(8,128)S(1)} %get-tuple-element.696), channel_id=1, source_target_pairs={{0,1},{1,2},{2,3},{3,0},{4,5},{5,6},{6,7},{7,4},{8,9},{9,10},{10,1... | collective-permute-start | bytes 98312 | tf_op jit(solution)/shard_map/while/body/eval_jaxpr/ppermute | solution.py:24
  67.4 4.1 %collective-permute-start.1 = (f32[64,128]{1,0:T(8,128)S(1)}, f32[64,128]{1,0:T(8,128)S(1)}, u32[]{:S(2)}, u32[]{:S(2)}) collective-permute-start(f32[64,128]{1,0:T(8,128)S(1)} %get-tuple-element.697), channel_id=1, source_target_pairs={{1,0},{2,1},{3,2},{0,3},{5,4},{6,5},{7,6},{4,7},{9,8},{10,9},{11,1... | collective-permute-start | bytes 98312 | tf_op jit(solution)/shard_map/while/body/eval_jaxpr/ppermute | solution.py:27
  92.4 5.8 %collective-permute-start.5 = (f32[64,128]{1,0:T(8,128)S(1)}, f32[64,128]{1,0:T(8,128)S(1)}, u32[]{:S(2)}, u32[]{:S(2)}) collective-permute-start(f32[64,128]{1,0:T(8,128)S(1)} %get-tuple-element.576), channel_id=1, source_target_pairs={{0,1},{1,2},{2,3},{3,0},{4,5},{5,6},{6,7},{7,4},{8,9},{9,10},{10,1... | collective-permute-start | bytes 98312 | tf_op jit(solution)/shard_map/ppermute | solution.py:24
  95.3 4.0 %collective-permute-start.6 = (f32[64,128]{1,0:T(8,128)S(1)}, f32[64,128]{1,0:T(8,128)S(1)}, u32[]{:S(2)}, u32[]{:S(2)}) collective-permute-start(f32[64,128]{1,0:T(8,128)S(1)} %get-tuple-element.575), channel_id=1, source_target_pairs={{1,0},{2,1},{3,2},{0,3},{5,4},{6,5},{7,6},{4,7},{9,8},{10,9},{11,1... | collective-permute-start | bytes 98312 | tf_op jit(solution)/shard_map/ppermute | solution.py:27
  112.8 54.0 %copy-start.2 = (f32[1,9,384]{2,0,1:T(1,128)S(1)}, f32[1,9,384]{2,0,1:T(1,128)}, u32[]{:S(2)}) copy-start(f32[1,9,384]{2,0,1:T(1,128)} %param.35) | copy-start | bytes 41476
  112.8 5.8 %collective-permute-start.2 = (f32[64,128]{1,0:T(8,128)S(1)}, f32[64,128]{1,0:T(8,128)S(1)}, u32[]{:S(2)}, u32[]{:S(2)}) collective-permute-start(f32[64,128]{1,0:T(8,128)S(1)} %get-tuple-element.710), channel_id=1, source_target_pairs={{0,1},{1,2},{2,3},{3,0},{4,5},{5,6},{6,7},{7,4},{8,9},{9,10},{10,1... | collective-permute-start | bytes 98312 | tf_op jit(solution)/shard_map/while/body/eval_jaxpr/ppermute | solution.py:24
  112.9 5.9 %collective-permute-start.3 = (f32[64,128]{1,0:T(8,128)S(1)}, f32[64,128]{1,0:T(8,128)S(1)}, u32[]{:S(2)}, u32[]{:S(2)}) collective-permute-start(f32[64,128]{1,0:T(8,128)S(1)} %get-tuple-element.711), channel_id=1, source_target_pairs={{1,0},{2,1},{3,2},{0,3},{5,4},{6,5},{7,6},{4,7},{9,8},{10,9},{11,1... | collective-permute-start | bytes 98312 | tf_op jit(solution)/shard_map/while/body/eval_jaxpr/ppermute | solution.py:27
  139.7 5.8 %collective-permute-start.2 = (f32[64,128]{1,0:T(8,128)S(1)}, f32[64,128]{1,0:T(8,128)S(1)}, u32[]{:S(2)}, u32[]{:S(2)}) collective-permute-start(f32[64,128]{1,0:T(8,128)S(1)} %get-tuple-element.710), channel_id=1, source_target_pairs={{0,1},{1,2},{2,3},{3,0},{4,5},{5,6},{6,7},{7,4},{8,9},{9,10},{10,1... | collective-permute-start | bytes 98312 | tf_op jit(solution)/shard_map/while/body/eval_jaxpr/ppermute | solution.py:24
  141.7 4.3 %collective-permute-start.3 = (f32[64,128]{1,0:T(8,128)S(1)}, f32[64,128]{1,0:T(8,128)S(1)}, u32[]{:S(2)}, u32[]{:S(2)}) collective-permute-start(f32[64,128]{1,0:T(8,128)S(1)} %get-tuple-element.711), channel_id=1, source_target_pairs={{1,0},{2,1},{3,2},{0,3},{5,4},{6,5},{7,6},{4,7},{9,8},{10,9},{11,1... | collective-permute-start | bytes 98312 | tf_op jit(solution)/shard_map/while/body/eval_jaxpr/ppermute | solution.py:27
  186.2 8.0 %all-to-all-start.2 = ((f32[8,1,144]{2,1,0:T(1,128)}), f32[8,1,144]{2,1,0:T(1,128)S(1)}, u32[]{:S(2)}, u32[]{:S(2)}) async-start(f32[8,1,144]{2,1,0:T(1,128)} %reshape.258), calls=%async_computation.2 | async-start | bytes 16384 | tf_op jit(solution)/shard_map/all_to_all | solution.py:146
where the time goes:
time: 197 us; the launch traced here: 196 us
  blocking collectives  120 us (61%)
  starting transfers between devices  35.7 us (18%)
  waiting for transfers between devices  13.8 us (7%)
  matrix products  11.2 us (6%)
  other arithmetic  7.84 us (4%)
  local copies, waits for them, and re-layouts  5.78 us (3%)
    psum x6, blocking collectives, norm_sum(): return lax.psum(jnp.sum(values * values, axis=0), 'rve')  54.4 us
    psum x4, blocking collectives, sweep(): curvature_col = lax.psum(jnp.sum(direct * product, axis=0), 'rve')  47.6 us
    psum x1, blocking collectives, shards(): group_stress = lax.psum(part_stress, 'rve')  18.3 us
    ppermute x5, starting transfers between devices, with_halo(): lax.ppermute(lax.slice_in_dim(block, 0, width, axis=dim), axis, backward)  11.7 us
    ppermute x5, starting transfers between devices, with_halo(): lax.ppermute(lax.slice_in_dim(block, block.shape[dim] - width, None, axis...  7.7 us
    ppermute x5, waiting for transfers between devices, with_halo(): lax.ppermute(lax.slice_in_dim(block, block.shape[dim] - width, None, axis...  6.12 us
    all_to_all x1, starting transfers between devices, shards(): lax.all_to_all(flags_out, 'macro', split_axis=1, concat_axis=1, tiled=True)  5.17 us
    all_to_all x1, starting transfers between devices, shards(): lax.all_to_all(outgoing, 'macro', split_axis=1, concat_axis=1, tiled=True)  4.2 us
  transfers between devices with their start and end apart: 14, of which 10 were waited for; matrix products, arithmetic and copies ran while one was open for 7% of the time, Pallas kernels for 0%

commit v1 on v0

--- a/solution.py
+++ b/solution.py
@@ -136,7 +136,12 @@
     ).reshape(1, groups, capacity)
     incoming, flags_in = (
         lax.all_to_all(outgoing, "macro", split_axis=1, concat_axis=1, tiled=True),
-        lax.all_to_all(flags_out, "macro", split_axis=1, concat_axis=1, tiled=True),
+        jnp.concatenate(
+            lax.all_to_all(
+                jnp.stack(jnp.split(flags_out, lax.axis_size("macro"), axis=1)), "macro", 0, 0
+            ),
+            axis=1,
+        ),
     )
     strain = incoming.reshape(9, columns)
     flag_cols = flags_in.reshape(1, columns)

time: 197 us -> 200 us (1.015)
  local copies, waits for them, and re-layouts: 5.78 us -> 9.98 us
    unnamed x23 -> x30, local copies, waits for them, and re-layouts: 2.24 us -> 5.85 us
where the time goes in v1:
time: 200 us; the launch traced here: 199 us
  blocking collectives  120 us (60%)
  starting transfers between devices  35.7 us (18%)
  waiting for transfers between devices  13.8 us (7%)
  matrix products  10.4 us (5%)
  local copies, waits for them, and re-layouts  9.98 us (5%)
  other arithmetic  7.84 us (4%)
    psum x6, blocking collectives, norm_sum(): return lax.psum(jnp.sum(values * values, axis=0), 'rve')  54.4 us
    psum x4, blocking collectives, sweep(): curvature_col = lax.psum(jnp.sum(direct * product, axis=0), 'rve')  47.6 us
    psum x1, blocking collectives, shards(): group_stress = lax.psum(part_stress, 'rve')  18.3 us
    ppermute x5, starting transfers between devices, with_halo(): lax.ppermute(lax.slice_in_dim(block, 0, width, axis=dim), axis, backward)  11.7 us
    ppermute x5, starting transfers between devices, with_halo(): lax.ppermute(lax.slice_in_dim(block, block.shape[dim] - width, None, axis...  7.7 us
    ppermute x5, waiting for transfers between devices, with_halo(): lax.ppermute(lax.slice_in_dim(block, block.shape[dim] - width, None, axis...  6.12 us
    unnamed x30, local copies, waits for them, and re-layouts  5.85 us
    all_to_all x1, starting transfers between devices, shards(): lax.all_to_all(jnp.stack(jnp.split(flags_out, lax.axis_size('macro'), axi...  5.17 us
  transfers between devices with their start and end apart: 14, of which 10 were waited for; matrix products, arithmetic and copies ran while one was open for 7% of the time, Pallas kernels for 0%

profile of v1, /device:TPU:0, one launch (start us, length us, event | category | flops | bytes accessed | tf_op | source)
XLA Modules:
  0.0 199.2 jit_solution(13101435723796853879)
XLA Ops:
  7.3 5.2 %all-to-all-start.1 = ((f32[8,1,1,16]{3,2,1,0:T(1,128)}), f32[8,1,1,16]{3,2,1,0:T(1,128)S(1)}, u32[]{:S(2)}, u32[]{:S(2)}) async-start(f32[8,1,1,16]{3,2,1,0:T(1,128)} %constant_dynamic-update-slice_fusion), calls=%async_computation.1 | async-start | bytes 8192 | tf_op jit(solution)/shard_map/all_to_all | solution.py:140
  12.4 3.6 %collective-permute-start.4 = (f32[64,64]{1,0:T(8,128)}, f32[64,64]{1,0:T(8,128)S(1)}, u32[]{:S(2)}, u32[]{:S(2)}) collective-permute-start(f32[64,64]{1,0:T(8,128)} %bitcast.130), channel_id=1, source_target_pairs={{1,0},{2,1},{3,2},{0,3},{5,4},{6,5},{7,6},{4,7},{9,8},{10,9},{11,1... | collective-permute-start | bytes 49160 | tf_op jit(solution)/shard_map/ppermute | solution.py:15
  18.2 1.5 convolution_bitcast_fusion.4
  21.7 4.2 %all-to-all-start = ((f32[8,1,144]{2,1,0:T(1,128)}), f32[8,1,144]{2,1,0:T(1,128)S(1)}, u32[]{:S(2)}, u32[]{:S(2)}) async-start(f32[8,1,144]{2,1,0:T(1,128)} %reshape.241), calls=%async_computation | async-start | bytes 16384 | tf_op jit(solution)/shard_map/all_to_all | solution.py:138
  27.5 3.1 %all-to-all-done = f32[8,1,144]{2,1,0:T(1,128)S(1)} async-done(((f32[8,1,144]{2,1,0:T(1,128)}), f32[8,1,144]{2,1,0:T(1,128)S(1)}, u32[]{:S(2)}, u32[]{:S(2)}) %all-to-all-start) | async-done | bytes 4640 | tf_op jit(solution)/shard_map/all_to_all | solution.py:138
  32.7 8.8 %psum.65 = f32[128]{0:T(128)S(1)} all-reduce(f32[128]{0:T(128)S(1)} %get-tuple-element.577), channel_id=1, replica_groups=mesh['macro'=8,'rve'=4] {'rve'}, use_global_device_ids=true, to_apply=%region_2.3 | all-reduce | flops 128 | bytes 1024 | tf_op jit(solution)/shard_map/psum | solution.py:59
  41.7 54.1 %while.46 = (s32[]{:T(128)}, f32[384,128]{1,0:T(8,128)S(1)}, f32[384,128]{1,0:T(8,128)S(1)}, f32[384,128]{1,0:T(8,128)S(1)}, f32[128]{0:T(128)S(1)}, /*index=5*/...) while((s32[]{:T(128)}, f32[384,128]{1,0:T(8,128)S(1)}, ...), condition=%wide.region_8.9_spmd.clone, body=%wide.region_3.8_spmd.clone.sunk | while | flops 240042496 | bytes 3879119 | solution.py:116
  41.8 1.6 collective-permute-start
  43.3 2.3 %collective-permute-start.1 = (f32[64,128]{1,0:T(8,128)S(1)}, f32[64,128]{1,0:T(8,128)S(1)}, u32[]{:S(2)}, u32[]{:S(2)}) collective-permute-start(f32[64,128]{1,0:T(8,128)S(1)} %get-tuple-element.697), channel_id=1, source_target_pairs={{1,0},{2,1},{3,2},{0,3},{5,4},{6,5},{7,6},{4,7},{9,8},{10,9},{11,1... | collective-permute-start | bytes 98312 | tf_op jit(solution)/shard_map/while/body/eval_jaxpr/ppermute | solution.py:27
  46.3 1.3 collective-permute-done
  48.1 11.9 %psum.76 = f32[128]{0:T(128)S(1)} all-reduce(f32[128]{0:T(128)S(1)} %multiply_reduce_fusion.10), channel_id=1, replica_groups=mesh['macro'=8,'rve'=4] {'rve'}, use_global_device_ids=true, to_apply=%region_5.5 | all-reduce | flops 128 | bytes 1024 | tf_op jit(solution)/shard_map/while/body/eval_jaxpr/psum | solution.py:107
  60.3 8.4 %psum.77 = f32[128]{0:T(128)S(1)} all-reduce(f32[128]{0:T(128)S(1)} %get-tuple-element.700), channel_id=1, replica_groups=mesh['macro'=8,'rve'=4] {'rve'}, use_global_device_ids=true, to_apply=%region_7.7 | all-reduce | flops 128 | bytes 1024 | tf_op jit(solution)/shard_map/while/body/eval_jaxpr/psum | solution.py:59
  68.8 2.0 %collective-permute-start = (f32[64,128]{1,0:T(8,128)S(1)}, f32[64,128]{1,0:T(8,128)S(1)}, u32[]{:S(2)}, u32[]{:S(2)}) collective-permute-start(f32[64,128]{1,0:T(8,128)S(1)} %get-tuple-element.696), channel_id=1, source_target_pairs={{0,1},{1,2},{2,3},{3,0},{4,5},{5,6},{6,7},{7,4},{8,9},{9,10},{10,1... | collective-permute-start | bytes 98312 | tf_op jit(solution)/shard_map/while/body/eval_jaxpr/ppermute | solution.py:24
  70.8 1.9 collective-permute-start.1
  73.3 1.3 collective-permute-done
  75.2 11.8 %psum.76 = f32[128]{0:T(128)S(1)} all-reduce(f32[128]{0:T(128)S(1)} %multiply_reduce_fusion.10), channel_id=1, replica_groups=mesh['macro'=8,'rve'=4] {'rve'}, use_global_device_ids=true, to_apply=%region_5.5 | all-reduce | flops 128 | bytes 1024 | tf_op jit(solution)/shard_map/while/body/eval_jaxpr/psum | solution.py:107
  87.3 8.4 %psum.77 = f32[128]{0:T(128)S(1)} all-reduce(f32[128]{0:T(128)S(1)} %get-tuple-element.700), channel_id=1, replica_groups=mesh['macro'=8,'rve'=4] {'rve'}, use_global_device_ids=true, to_apply=%region_7.7 | all-reduce | flops 128 | bytes 1024 | tf_op jit(solution)/shard_map/while/body/eval_jaxpr/psum | solution.py:59
  95.8 2.0 %collective-permute-start.5 = (f32[64,128]{1,0:T(8,128)S(1)}, f32[64,128]{1,0:T(8,128)S(1)}, u32[]{:S(2)}, u32[]{:S(2)}) collective-permute-start(f32[64,128]{1,0:T(8,128)S(1)} %get-tuple-element.576), channel_id=1, source_target_pairs={{0,1},{1,2},{2,3},{3,0},{4,5},{5,6},{6,7},{7,4},{8,9},{9,10},{10,1... | collective-permute-start | bytes 98312 | tf_op jit(solution)/shard_map/ppermute | solution.py:24
  98.7 1.9 collective-permute-start.6
  104.1 12.1 %psum.66 = f32[128]{0:T(128)S(1)} all-reduce(f32[128]{0:T(128)S(1)} %get-tuple-element.566), channel_id=1, replica_groups=mesh['macro'=8,'rve'=4] {'rve'}, use_global_device_ids=true, to_apply=%region_10.11 | all-reduce | flops 128 | bytes 1024 | tf_op jit(solution)/shard_map/psum | solution.py:59
  116.2 54.0 %while.47 = (s32[]{:T(128)}, f32[384,128]{1,0:T(8,128)S(1)}, f32[384,128]{1,0:T(8,128)S(1)}, f32[384,128]{1,0:T(8,128)S(1)}, f32[128]{0:T(128)S(1)}, /*index=5*/...) while((s32[]{:T(128)}, f32[384,128]{1,0:T(8,128)S(1)}, ...), condition=%wide.region_16.17_spmd.clone, body=%wide.region_11.16_spmd.clone.sunk | while | flops 239845888 | bytes 4268231 | solution.py:116
  116.3 3.8 %collective-permute-start.3 = (f32[64,128]{1,0:T(8,128)S(1)}, f32[64,128]{1,0:T(8,128)S(1)}, u32[]{:S(2)}, u32[]{:S(2)}) collective-permute-start(f32[64,128]{1,0:T(8,128)S(1)} %get-tuple-element.711), channel_id=1, source_target_pairs={{1,0},{2,1},{3,2},{0,3},{5,4},{6,5},{7,6},{4,7},{9,8},{10,9},{11,1... | collective-permute-start | bytes 98312 | tf_op jit(solution)/shard_map/while/body/eval_jaxpr/ppermute | solution.py:27
  122.4 12.0 %psum.78 = f32[128]{0:T(128)S(1)} all-reduce(f32[128]{0:T(128)S(1)} %multiply_reduce_fusion.12), channel_id=1, replica_groups=mesh['macro'=8,'rve'=4] {'rve'}, use_global_device_ids=true, to_apply=%region_13.13 | all-reduce | flops 128 | bytes 1024 | tf_op jit(solution)/shard_map/while/body/eval_jaxpr/psum | solution.py:107
  134.6 8.4 %psum.79 = f32[128]{0:T(128)S(1)} all-reduce(f32[128]{0:T(128)S(1)} %get-tuple-element.714), channel_id=1, replica_groups=mesh['macro'=8,'rve'=4] {'rve'}, use_global_device_ids=true, to_apply=%region_15.15 | all-reduce | flops 128 | bytes 1024 | tf_op jit(solution)/shard_map/while/body/eval_jaxpr/psum | solution.py:59
  143.1 2.0 %collective-permute-start.2 = (f32[64,128]{1,0:T(8,128)S(1)}, f32[64,128]{1,0:T(8,128)S(1)}, u32[]{:S(2)}, u32[]{:S(2)}) collective-permute-start(f32[64,128]{1,0:T(8,128)S(1)} %get-tuple-element.710), channel_id=1, source_target_pairs={{0,1},{1,2},{2,3},{3,0},{4,5},{5,6},{6,7},{7,4},{8,9},{9,10},{10,1... | collective-permute-start | bytes 98312 | tf_op jit(solution)/shard_map/while/body/eval_jaxpr/ppermute | solution.py:24
  145.1 1.9 collective-permute-start.3
  147.6 1.3 collective-permute-done.2
  149.6 11.9 %psum.78 = f32[128]{0:T(128)S(1)} all-reduce(f32[128]{0:T(128)S(1)} %multiply_reduce_fusion.12), channel_id=1, replica_groups=mesh['macro'=8,'rve'=4] {'rve'}, use_global_device_ids=true, to_apply=%region_13.13 | all-reduce | flops 128 | bytes 1024 | tf_op jit(solution)/shard_map/while/body/eval_jaxpr/psum | solution.py:107
  161.7 8.4 %psum.79 = f32[128]{0:T(128)S(1)} all-reduce(f32[128]{0:T(128)S(1)} %get-tuple-element.714), channel_id=1, replica_groups=mesh['macro'=8,'rve'=4] {'rve'}, use_global_device_ids=true, to_apply=%region_15.15 | all-reduce | flops 128 | bytes 1024 | tf_op jit(solution)/shard_map/while/body/eval_jaxpr/psum | solution.py:59
  170.6 18.3 %psum.67 = f32[9,8,16]{2,0,1:T(8,128)S(1)} all-reduce(f32[9,8,16]{2,0,1:T(8,128)S(1)} %copy.102), channel_id=1, replica_groups=mesh['macro'=8,'rve'=4] {'rve'}, use_global_device_ids=true, to_apply=%region_17.18 | all-reduce | flops 1152 | bytes 9216 | tf_op jit(solution)/shard_map/psum | solution.py:150
  189.5 3.3 %all-to-all-start.2 = ((f32[8,1,144]{2,1,0:T(1,128)}), f32[8,1,144]{2,1,0:T(1,128)S(1)}, u32[]{:S(2)}, u32[]{:S(2)}) async-start(f32[8,1,144]{2,1,0:T(1,128)} %reshape.243), calls=%async_computation.2 | async-start | bytes 16384 | tf_op jit(solution)/shard_map/all_to_all | solution.py:151
  193.6 3.9 %all-to-all-done.2 = f32[8,1,144]{2,1,0:T(1,128)S(1)} async-done(((f32[8,1,144]{2,1,0:T(1,128)}), f32[8,1,144]{2,1,0:T(1,128)S(1)}, u32[]{:S(2)}, u32[]{:S(2)}) %all-to-all-start.2) | async-done | bytes 4640 | tf_op jit(solution)/shard_map/all_to_all | solution.py:151
  (126 shorter events, 29.6 us)
Async XLA Ops:
  0.6 16.8 %copy-start = (f32[1,6,2,64,64]{4,3,2,1,0:T(8,128)S(1)}, f32[1,6,2,64,64]{4,3,2,1,0:T(8,128)}, u32[]{:S(2)}) copy-start(f32[1,6,2,64,64]{4,3,2,1,0:T(8,128)} %param.31) | copy-start | bytes 589828
  7.3 14.4 %all-to-all-start.1 = ((f32[8,1,1,16]{3,2,1,0:T(1,128)}), f32[8,1,1,16]{3,2,1,0:T(1,128)S(1)}, u32[]{:S(2)}, u32[]{:S(2)}) async-start(f32[8,1,1,16]{3,2,1,0:T(1,128)} %constant_dynamic-update-slice_fusion), calls=%async_computation.1 | async-start | bytes 8192 | tf_op jit(solution)/shard_map/all_to_all | solution.py:140
  12.4 29.1 %collective-permute-start.4 = (f32[64,64]{1,0:T(8,128)}, f32[64,64]{1,0:T(8,128)S(1)}, u32[]{:S(2)}, u32[]{:S(2)}) collective-permute-start(f32[64,64]{1,0:T(8,128)} %bitcast.130), channel_id=1, source_target_pairs={{1,0},{2,1},{3,2},{0,3},{5,4},{6,5},{7,6},{4,7},{9,8},{10,9},{11,1... | collective-permute-start | bytes 49160 | tf_op jit(solution)/shard_map/ppermute | solution.py:15
  19.8 0.7 copy-start.4
  19.9 0.8 copy-start.6
  19.9 6.0 %copy-start.3 = (f32[1,64,64]{2,1,0:T(8,128)S(1)}, f32[1,64,64]{2,1,0:T(8,128)}, u32[]{:S(2)}) copy-start(f32[1,64,64]{2,1,0:T(8,128)} %param.33) | copy-start | bytes 49156
  19.9 6.2 %copy-start.5 = (f32[1,384]{1,0:T(1,128)S(1)}, f32[1,384]{1,0:T(1,128)}, u32[]{:S(2)}) copy-start(f32[1,384]{1,0:T(1,128)} %param.30) | copy-start | bytes 4612
  19.9 12.2 %copy-start.1 = (f32[1,9,384]{2,0,1:T(1,128)S(1)}, f32[1,9,384]{2,0,1:T(1,128)}, u32[]{:S(2)}) copy-start(f32[1,9,384]{2,0,1:T(1,128)} %param.34) | copy-start | bytes 41476
  21.7 8.9 %all-to-all-start = ((f32[8,1,144]{2,1,0:T(1,128)}), f32[8,1,144]{2,1,0:T(1,128)S(1)}, u32[]{:S(2)}, u32[]{:S(2)}) async-start(f32[8,1,144]{2,1,0:T(1,128)} %reshape.241), calls=%async_computation | async-start | bytes 16384 | tf_op jit(solution)/shard_map/all_to_all | solution.py:138
  41.8 5.8 %collective-permute-start = (f32[64,128]{1,0:T(8,128)S(1)}, f32[64,128]{1,0:T(8,128)S(1)}, u32[]{:S(2)}, u32[]{:S(2)}) collective-permute-start(f32[64,128]{1,0:T(8,128)S(1)} %get-tuple-element.696), channel_id=1, source_target_pairs={{0,1},{1,2},{2,3},{3,0},{4,5},{5,6},{6,7},{7,4},{8,9},{9,10},{10,1... | collective-permute-start | bytes 98312 | tf_op jit(solution)/shard_map/while/body/eval_jaxpr/ppermute | solution.py:24
  43.3 4.4 %collective-permute-start.1 = (f32[64,128]{1,0:T(8,128)S(1)}, f32[64,128]{1,0:T(8,128)S(1)}, u32[]{:S(2)}, u32[]{:S(2)}) collective-permute-start(f32[64,128]{1,0:T(8,128)S(1)} %get-tuple-element.697), channel_id=1, source_target_pairs={{1,0},{2,1},{3,2},{0,3},{5,4},{6,5},{7,6},{4,7},{9,8},{10,9},{11,1... | collective-permute-start | bytes 98312 | tf_op jit(solution)/shard_map/while/body/eval_jaxpr/ppermute | solution.py:27
  68.8 5.8 %collective-permute-start = (f32[64,128]{1,0:T(8,128)S(1)}, f32[64,128]{1,0:T(8,128)S(1)}, u32[]{:S(2)}, u32[]{:S(2)}) collective-permute-start(f32[64,128]{1,0:T(8,128)S(1)} %get-tuple-element.696), channel_id=1, source_target_pairs={{0,1},{1,2},{2,3},{3,0},{4,5},{5,6},{6,7},{7,4},{8,9},{9,10},{10,1... | collective-permute-start | bytes 98312 | tf_op jit(solution)/shard_map/while/body/eval_jaxpr/ppermute | solution.py:24
  70.8 4.1 %collective-permute-start.1 = (f32[64,128]{1,0:T(8,128)S(1)}, f32[64,128]{1,0:T(8,128)S(1)}, u32[]{:S(2)}, u32[]{:S(2)}) collective-permute-start(f32[64,128]{1,0:T(8,128)S(1)} %get-tuple-element.697), channel_id=1, source_target_pairs={{1,0},{2,1},{3,2},{0,3},{5,4},{6,5},{7,6},{4,7},{9,8},{10,9},{11,1... | collective-permute-start | bytes 98312 | tf_op jit(solution)/shard_map/while/body/eval_jaxpr/ppermute | solution.py:27
  95.8 5.8 %collective-permute-start.5 = (f32[64,128]{1,0:T(8,128)S(1)}, f32[64,128]{1,0:T(8,128)S(1)}, u32[]{:S(2)}, u32[]{:S(2)}) collective-permute-start(f32[64,128]{1,0:T(8,128)S(1)} %get-tuple-element.576), channel_id=1, source_target_pairs={{0,1},{1,2},{2,3},{3,0},{4,5},{5,6},{6,7},{7,4},{8,9},{9,10},{10,1... | collective-permute-start | bytes 98312 | tf_op jit(solution)/shard_map/ppermute | solution.py:24
  98.7 4.0 %collective-permute-start.6 = (f32[64,128]{1,0:T(8,128)S(1)}, f32[64,128]{1,0:T(8,128)S(1)}, u32[]{:S(2)}, u32[]{:S(2)}) collective-permute-start(f32[64,128]{1,0:T(8,128)S(1)} %get-tuple-element.575), channel_id=1, source_target_pairs={{1,0},{2,1},{3,2},{0,3},{5,4},{6,5},{7,6},{4,7},{9,8},{10,9},{11,1... | collective-permute-start | bytes 98312 | tf_op jit(solution)/shard_map/ppermute | solution.py:27
  116.2 54.0 %copy-start.2 = (f32[1,9,384]{2,0,1:T(1,128)S(1)}, f32[1,9,384]{2,0,1:T(1,128)}, u32[]{:S(2)}) copy-start(f32[1,9,384]{2,0,1:T(1,128)} %param.35) | copy-start | bytes 41476
  116.2 5.8 %collective-permute-start.2 = (f32[64,128]{1,0:T(8,128)S(1)}, f32[64,128]{1,0:T(8,128)S(1)}, u32[]{:S(2)}, u32[]{:S(2)}) collective-permute-start(f32[64,128]{1,0:T(8,128)S(1)} %get-tuple-element.710), channel_id=1, source_target_pairs={{0,1},{1,2},{2,3},{3,0},{4,5},{5,6},{6,7},{7,4},{8,9},{9,10},{10,1... | collective-permute-start | bytes 98312 | tf_op jit(solution)/shard_map/while/body/eval_jaxpr/ppermute | solution.py:24
  116.3 5.9 %collective-permute-start.3 = (f32[64,128]{1,0:T(8,128)S(1)}, f32[64,128]{1,0:T(8,128)S(1)}, u32[]{:S(2)}, u32[]{:S(2)}) collective-permute-start(f32[64,128]{1,0:T(8,128)S(1)} %get-tuple-element.711), channel_id=1, source_target_pairs={{1,0},{2,1},{3,2},{0,3},{5,4},{6,5},{7,6},{4,7},{9,8},{10,9},{11,1... | collective-permute-start | bytes 98312 | tf_op jit(solution)/shard_map/while/body/eval_jaxpr/ppermute | solution.py:27
  143.1 5.8 %collective-permute-start.2 = (f32[64,128]{1,0:T(8,128)S(1)}, f32[64,128]{1,0:T(8,128)S(1)}, u32[]{:S(2)}, u32[]{:S(2)}) collective-permute-start(f32[64,128]{1,0:T(8,128)S(1)} %get-tuple-element.710), channel_id=1, source_target_pairs={{0,1},{1,2},{2,3},{3,0},{4,5},{5,6},{6,7},{7,4},{8,9},{9,10},{10,1... | collective-permute-start | bytes 98312 | tf_op jit(solution)/shard_map/while/body/eval_jaxpr/ppermute | solution.py:24
  145.1 4.3 %collective-permute-start.3 = (f32[64,128]{1,0:T(8,128)S(1)}, f32[64,128]{1,0:T(8,128)S(1)}, u32[]{:S(2)}, u32[]{:S(2)}) collective-permute-start(f32[64,128]{1,0:T(8,128)S(1)} %get-tuple-element.711), channel_id=1, source_target_pairs={{1,0},{2,1},{3,2},{0,3},{5,4},{6,5},{7,6},{4,7},{9,8},{10,9},{11,1... | collective-permute-start | bytes 98312 | tf_op jit(solution)/shard_map/while/body/eval_jaxpr/ppermute | solution.py:27
  189.5 8.0 %all-to-all-start.2 = ((f32[8,1,144]{2,1,0:T(1,128)}), f32[8,1,144]{2,1,0:T(1,128)S(1)}, u32[]{:S(2)}, u32[]{:S(2)}) async-start(f32[8,1,144]{2,1,0:T(1,128)} %reshape.243), calls=%async_computation.2 | async-start | bytes 16384 | tf_op jit(solution)/shard_map/all_to_all | solution.py:151
